TPU v7x, 512 devices: a whole 4x4x16 slice. The times are simulated.
512 devices in a mesh: range: 32 (over x, z_hi, y), ping: 16 (over z_lo, core).
Axes of the slice: x: 4, y: 4, z: 16 (z_hi: 2, z_lo: 8; z = z_hi * 8 + z_lo), core: 2. Of those that a mesh axis runs over, the one named last changes fastest.
Arguments:
- echoes: bfloat16 [128, 32, 4096], P('ping', None, 'range'), may hold values from -6 to 6
- band_offset: int32 [128], P('ping'), may hold values from -128 to 64
- sway_delay: float32 [128, 32], P('ping'), may hold values from 0 to 1
- channel_gain: float32 [128, 32], P('ping'), may hold values from 0.5 to 2
- track_bin: int32 [128], P('ping'), may hold values from 0 to 2047
Outputs:
- image_real: float32 [2048, 4096], P('ping', 'range')
- image_imag: float32 [2048, 4096], P('ping', 'range')
All inputs are finite; a program needn't handle non-finite values.
Results may differ from a plain program's by a relative error of at most 0.017.
Values may be sent and summed in bfloat16 or wider, within the bound.
A program may use at most 64 MiB of HBM per device.

v0:
```python
import math

import jax
import jax.numpy as jnp
from jax import lax
from jax.sharding import PartitionSpec as P

X = 2048
BAND = 64
HALO = 128


def extended(block, sides, width):
    for axis, dim in sides:
        count = lax.axis_size(axis)
        forward = [(i, i + 1) for i in range(count - 1)]
        backward = [(target, source) for source, target in forward]
        low = lax.ppermute(
            lax.slice_in_dim(block, block.shape[dim] - width, None, axis=dim), axis, forward
        )
        high = lax.ppermute(lax.slice_in_dim(block, 0, width, axis=dim), axis, backward)
        block = jnp.concatenate([low, block, high], axis=dim)
    return block


def make_taps(sway_delay, channel_gain):
    kpos = jnp.arange(BAND, dtype=jnp.float32)
    shift = kpos - (BAND / 2 - 1) - sway_delay[..., None]
    window = 0.5 - 0.5 * jnp.cos(2.0 * math.pi * (kpos + 0.5) / BAND)
    return jnp.sinc(shift) * window * channel_gain[..., None]


def compensate(padded, offsets, taps, samples):
    padded = padded.astype(jnp.float32)
    ping_count, channels, _ = padded.shape

    def pick(row, shift):
        return lax.dynamic_slice_in_dim(row, shift + HALO, samples + BAND - 1, 1)

    windows = jax.vmap(pick)(padded, offsets)
    lhs = windows.reshape(1, ping_count * channels, samples + BAND - 1)
    rhs = taps.reshape(ping_count * channels, 1, BAND).astype(jnp.float32)
    result = lax.conv_general_dilated(
        lhs,
        rhs,
        (1,),
        "VALID",
        dimension_numbers=("NCH", "OIH", "NCH"),
        feature_group_count=ping_count * channels,
        precision=lax.Precision.HIGHEST,
    )
    return result.reshape(ping_count, channels, samples).astype(jnp.bfloat16)


def make_steer(first_row, row_count, track, channels, scaling, spread):
    xpos = jnp.asarray(first_row).astype(jnp.float32) + jnp.arange(row_count, dtype=jnp.float32)
    centre = (
        track.astype(jnp.float32)[:, None] + 0.5 * jnp.arange(channels, dtype=jnp.float32)[None, :]
    )
    centre = centre.reshape(-1)
    diff = xpos[:, None] - centre[None, :]
    dist = diff * (8.0 / X)
    weight = jnp.exp(-0.5 * dist * dist) * scaling
    phase = diff * diff * (math.pi / spread)
    return (
        (weight * jnp.cos(phase)).astype(jnp.bfloat16),
        (weight * jnp.sin(phase)).astype(jnp.bfloat16),
    )


def image_rows(first_row, row_count, track, columns, channels, scaling, spread):
    block_rows = math.gcd(row_count, 256)
    block_count = row_count // block_rows

    def one_block(block_index):
        steer_real, steer_imag = make_steer(
            first_row + block_index * block_rows, block_rows, track, channels, scaling, spread
        )
        part_real = jnp.dot(steer_real, columns, preferred_element_type=jnp.float32)
        part_imag = jnp.dot(steer_imag, columns, preferred_element_type=jnp.float32)
        return jnp.concatenate([part_real, part_imag], axis=1)

    blocks = lax.map(one_block, jnp.arange(block_count, dtype=jnp.int32))
    return blocks.reshape(row_count, 2 * columns.shape[1])


def shards(echoes, band_offset, sway_delay, channel_gain, track_bin):
    ping_count, channels, samples = echoes.shape
    taps = make_taps(sway_delay, channel_gain)
    padded = extended(echoes, (("range", 2),), HALO)
    compensated = compensate(padded, band_offset, taps, samples)
    columns = compensated.reshape(ping_count * channels, samples)
    scaling = 1.0 / math.sqrt(lax.axis_size("ping") * ping_count * channels)
    band_share = samples / (samples * lax.axis_size("range"))
    spread = 0.5 * X * (1.0 + (lax.axis_index("range").astype(jnp.float32) + 0.5) * band_share)
    whole = image_rows(0, X, track_bin, columns, channels, scaling, spread)
    image = lax.psum_scatter(
        whole.astype(jnp.bfloat16), "ping", scatter_dimension=0, tiled=True
    ).astype(jnp.float32)
    return (image[:, :samples], image[:, samples:])


def solution(mesh):
    return jax.shard_map(
        shards,
        mesh=mesh,
        in_specs=(P("ping", None, "range"), P("ping"), P("ping", None), P("ping", None), P("ping")),
        out_specs=(P("ping", "range"), P("ping", "range")),
        check_vma=False,
    )
```

profile of v0, /device:TPU:6, one launch (start us, length us, event | category | flops | bytes accessed | tf_op | source)
XLA Modules:
  0.0 184.7 jit_solution(2065015804909233254)
XLA Ops:
  7.2 3.5 %collective-permute-start = (bf16[8,32,128]{2,1,0:T(8,128)(2,1)}, bf16[8,32,128]{2,1,0:T(8,128)(2,1)S(1)}, u32[]{:S(2)}, u32[]{:S(2)}) collective-permute-start(bf16[8,32,128]{2,1,0:T(8,128)(2,1)} %param.7), channel_id=1, source_target_pairs={{0,16},{16,32},{32,48},{48,64},{64,80},{80,96},{96,112},{112,128},... | collective-permute-start | bytes 196616 | tf_op jit(solution)/shard_map/ppermute | solution.py:18
  10.7 16.9 %collective-permute-start.1 = (bf16[8,32,128]{2,1,0:T(8,128)(2,1)}, bf16[8,32,128]{2,1,0:T(8,128)(2,1)S(1)}, u32[]{:S(2)}, u32[]{:S(2)}) collective-permute-start(bf16[8,32,128]{2,1,0:T(8,128)(2,1)} %param.7), channel_id=1, source_target_pairs={{16,0},{32,16},{48,32},{64,48},{80,64},{96,80},{112,96},{128,112},... | collective-permute-start | bytes 196616 | tf_op jit(solution)/shard_map/ppermute | solution.py:21
  27.6 0.8 mul.258
  28.4 0.8 sub.81
  29.2 0.7 fusion.60
  29.8 0.2 fusion.39
  30.0 0.5 copy-done.1
  30.6 0.5 copy.25
  31.1 1.7 gather_fusion
  32.8 0.3 copy.26
  33.1 0.2 copy.27
  33.3 1.0 convolution_convert_fusion
  34.3 0.1 copy.29
  34.4 29.3 %while.12 = (s32[]{:T(128)}, bf16[8,256,256]{1,2,0:T(8,128)(2,1)S(1)}, s32[8]{0:T(128)S(1)}, f32[8,1]{0,1:T(1,128)S(1)}, f32[]{:T(128)}, /*index=5*/bf16[256,128]{1,0:T(8,128)(2,1)S(1)}, s32[]{:T(128)}, s32[1]{0:T(128)}) while((s32[]{:T(128)}, bf16[8,256,256]{1,2,0:T(8,128)(2,1)S(1)}, s32[8]{0:T(128)S(1)}, f32[8,1]{0,1:T(1,128)S(1)}, ...), condition=%wide.region_1.2_spmd, body=%wide.region_0.1_spmd.sunk | while | flops 34996772 | bytes 532901 | solution.py:83
  34.4 0.6 dynamic_slice.8
  35.7 0.1 add.305
  35.8 1.2 fusion.76
  36.9 1.1 fusion.77
  38.1 0.6 dynamic_slice.8
  39.4 0.1 add.305
  39.4 1.2 fusion.76
  40.6 1.1 fusion.77
  41.8 0.6 dynamic_slice.8
  43.0 0.1 add.305
  43.1 1.2 fusion.76
  44.3 1.1 fusion.77
  45.4 0.6 dynamic_slice.8
  46.7 0.1 add.305
  46.8 1.2 fusion.76
  47.9 1.1 fusion.77
  49.1 0.6 dynamic_slice.8
  50.4 0.1 add.305
  50.4 1.2 fusion.76
  51.6 1.1 fusion.77
  52.8 0.6 dynamic_slice.8
  54.0 0.1 add.305
  54.1 1.2 fusion.76
  55.3 1.1 fusion.77
  56.4 0.6 dynamic_slice.8
  57.7 0.1 add.305
  57.8 1.2 fusion.76
  58.9 1.1 fusion.77
  60.1 0.6 dynamic_slice.8
  61.4 1.2 fusion.76
  62.6 1.1 fusion.77
  63.8 1.3 copy.30
  65.1 111.3 %reduce-scatter.2.cloned.1.call-done = bf16[128,256]{1,0:T(8,128)(2,1)} async-done(((bf16[2048,256]{1,0:T(8,128)(2,1)}), bf16[128,256]{1,0:T(8,128)(2,1)}) %reduce-scatter.2.cloned.1.call-update) | async-done | bytes 65552 | tf_op jit(solution)/shard_map/reduce_scatter | solution.py:97
  176.4 1.4 fusion.61
  (45 shorter events, 1.1 us)
Async XLA Ops:
  7.2 23.4 %copy-start = (bf16[8,32,128]{2,1,0:T(8,128)(2,1)S(1)}, bf16[8,32,128]{2,1,0:T(8,128)(2,1)}, u32[]{:S(2)}) copy-start(bf16[8,32,128]{2,1,0:T(8,128)(2,1)} %param.7) | copy-start | bytes 196612
  7.2 169.2 %reduce-scatter.2.cloned.1.call-start = ((), (), s32[]{:S(2)}) async-start(), calls=%async_computation.1 | async-start | bytes 1114112 | tf_op jit(solution)/shard_map/reduce_scatter | solution.py:97
  7.2 23.3 %collective-permute-start = (bf16[8,32,128]{2,1,0:T(8,128)(2,1)}, bf16[8,32,128]{2,1,0:T(8,128)(2,1)S(1)}, u32[]{:S(2)}, u32[]{:S(2)}) collective-permute-start(bf16[8,32,128]{2,1,0:T(8,128)(2,1)} %param.7), channel_id=1, source_target_pairs={{0,16},{16,32},{32,48},{48,64},{64,80},{80,96},{96,112},{112,128},... | collective-permute-start | bytes 196616 | tf_op jit(solution)/shard_map/ppermute | solution.py:18
  10.7 19.8 %collective-permute-start.1 = (bf16[8,32,128]{2,1,0:T(8,128)(2,1)}, bf16[8,32,128]{2,1,0:T(8,128)(2,1)S(1)}, u32[]{:S(2)}, u32[]{:S(2)}) collective-permute-start(bf16[8,32,128]{2,1,0:T(8,128)(2,1)} %param.7), channel_id=1, source_target_pairs={{16,0},{32,16},{48,32},{64,48},{80,64},{96,80},{112,96},{128,112},... | collective-permute-start | bytes 196616 | tf_op jit(solution)/shard_map/ppermute | solution.py:21
  29.8 0.7 copy-start.1
Sparse Core Ops, SparseCore 0:
  65.2 111.1 reduce-scatter.1
where the time goes:
time: 186 us; the launch traced here: 185 us
  waiting for transfers between devices  111 us (60%)
  starting transfers between devices  20.4 us (11%)
  matrix products  19.4 us (10%)
  between operations  14.2 us (8%)
  local copies, waits for them, and re-layouts  12.8 us (7%)
  loops' own time  4.8 us (3%)
    reduce_scatter x1, waiting for transfers between devices, shards(): lax.psum_scatter(whole.astype(jnp.bfloat16), 'ping', scatter_dimension=0,...  111 us
    ppermute x1, starting transfers between devices, extended(): lax.ppermute(lax.slice_in_dim(block, 0, width, axis=dim), axis, backward)  16.9 us
    dot_general x8, matrix products, one_block(): part_imag = jnp.dot(steer_imag, columns, preferred_element_type=jnp.float32)  9.21 us
    dot_general x8, matrix products, one_block(): part_real = jnp.dot(steer_real, columns, preferred_element_type=jnp.float32)  9.19 us
    another operation x1, loops' own time, image_rows(): blocks = lax.map(one_block, jnp.arange(block_count, dtype=jnp.int32))  4.8 us
    dynamic_slice x8, local copies, waits for them, and re-layouts, image_rows(): blocks = lax.map(one_block, jnp.arange(block_count, dtype=jnp.int32))  4.64 us
  transfers between devices with their start and end apart: 3, of which 1 were waited for; matrix products, arithmetic and copies ran while one was open for 1% of the time, Pallas kernels for 0%

commit v1 on v0

v1 whole, which is shorter than its diff:
```python
import functools
import math

import jax
import jax.numpy as jnp
import numpy as np
from jax import lax
from jax.experimental import pallas as pl
from jax.experimental.pallas import tpu as pltpu
from jax.sharding import PartitionSpec as P

X = 2048
BAND = 64
HALO = 128
NR = 32
NP = 16
PD = 8
C = 32
RD = 128
PC = PD * C
ROWS = X // NP
NC = 2
PR = PC // NC
MESH = pl.DeviceIdType.MESH


def fit(fun, degree):
    nodes = 0.125 + 0.125 * np.cos(np.pi * (np.arange(400) + 0.5) / 400)
    series = np.polynomial.chebyshev.Chebyshev.fit(nodes, fun(nodes), degree, domain=[0.0, 0.25])
    return [float(c) for c in series.convert(kind=np.polynomial.Polynomial).coef]


COS = fit(lambda w: np.cos(2 * np.pi * np.sqrt(w)), 8)
SIN = fit(lambda w: np.sin(2 * np.pi * np.sqrt(w)) / np.sqrt(w), 7)
SINPI = fit(lambda w: np.sin(np.pi * np.sqrt(w)) / np.sqrt(w), 6)


def horner(coefs, w):
    value = jnp.full_like(w, coefs[-1])
    for c in coefs[-2::-1]:
        value = value * w + c
    return value


def sin_pi(u):
    u = jnp.minimum(u, 1.0 - u)
    return u * horner(SINPI, u * u)


def kernel(
    off_ref, track_ref, e_ref, sway_ref, gain_ref, re_ref, im_ref,
    halo, et, win, taps, gath, mine, steer, acc,
    hs, hr, ms, mr, ss, rs,
):
    r = lax.axis_index("range")
    g = lax.axis_index("ping")
    z, core = g // 2, g % 2
    half, pos = z // 4, z % 4
    other = (r, g + 1 - 2 * core)
    right = (r, jnp.minimum(g + 2, NP - 1))
    left = (r, jnp.maximum(g - 2, 0))
    across = (r, g + 8 - 16 * half)
    after = (jnp.minimum(r + 1, NR - 1), g)
    before = (jnp.maximum(r - 1, 0), g)

    barrier = pltpu.get_barrier_semaphore()
    for j in range(1, NP):
        pl.semaphore_signal(barrier, 1, device_id=(r, (g + j) % NP), device_id_type=MESH)

    @pl.when(r > 0)
    def _():
        pl.semaphore_signal(barrier, 1, device_id=before, device_id_type=MESH)

    @pl.when(r < NR - 1)
    def _():
        pl.semaphore_signal(barrier, 1, device_id=after, device_id_type=MESH)

    lane = lax.broadcasted_iota(jnp.int32, (8, PC), 1)
    ping = lane // C
    centre = lane % C
    for p in range(PD):
        centre = centre + jnp.where(ping == p, 2 * track_ref[p], 0)
    mine[g] = centre

    kpos = lax.broadcasted_iota(jnp.int32, (BAND, 1), 0).astype(jnp.float32)
    edge = sin_pi((kpos + 0.5) * (1.0 / BAND))
    edge = edge * edge
    kfull = lax.broadcasted_iota(jnp.int32, (BAND, 128), 0)
    odd = (kfull % 2).astype(jnp.float32)
    for b in range(2):
        sway = jnp.concatenate([sway_ref[4 * b + q : 4 * b + q + 1, :] for q in range(4)], axis=1)
        gain = jnp.concatenate([gain_ref[4 * b + q : 4 * b + q + 1, :] for q in range(4)], axis=1)
        top = sin_pi(sway) * (1.0 / math.pi)
        shift = kfull.astype(jnp.float32) - (BAND / 2 - 1) - sway
        sinc = jnp.where(shift == 0.0, 1.0, (1.0 - 2.0 * odd) * top / jnp.where(shift == 0.0, 1.0, shift))
        taps[b] = sinc * edge * gain

    pl.semaphore_wait(barrier, NP + 1 - 1 // (r + 1) - r // (NR - 1))

    def halo_copy(way, device):
        return pltpu.make_async_remote_copy(
            e_ref, halo.at[way], hs.at[way], hr.at[way], device_id=device, device_id_type=MESH
        )

    @pl.when(r < NR - 1)
    def _():
        halo_copy(0, after).start()

    @pl.when(r > 0)
    def _():
        halo_copy(1, before).start()

    def mine_copy(slot, j):
        return pltpu.make_async_remote_copy(
            mine.at[slot], mine.at[slot], ms.at[j], mr.at[slot], device_id=(r, (g + j) % NP), device_id_type=MESH
        )

    for j in range(1, NP):
        mine_copy(g, j).start()

    def lay(block, third):
        for b in range(2):
            et[b, third * RD : (third + 1) * RD, :] = block[b * 128 : (b + 1) * 128, :].astype(jnp.float32).T

    lay(e_ref, 1)

    full = (64 * 2 * (2 * r + 65)).astype(jnp.float32)
    turn = 1.0 / jnp.full((16, PC), full, jnp.float32)
    row = 2 * (ROWS * g + lax.broadcasted_iota(jnp.int32, (16, PC), 0))
    scale = 1.0 / math.sqrt(NP * PC)

    def build(slot):
        def rows(i, carry):
            centres = jnp.concatenate([mine[slot], mine[slot]], axis=0)
            m = (row + 32 * i - centres).astype(jnp.float32)
            m2 = m * m
            u = (m2 - jnp.floor(m2 * turn + 0.5) * full) * turn
            w = u * u
            weight = jnp.exp(m2 * (-1.0 / (8.0 * 65536.0))) * scale
            at = pl.multiple_of(16 * i, 16)
            steer[slot, pl.ds(at, 16), :] = (weight * horner(COS, w)).astype(jnp.bfloat16)
            at = pl.multiple_of(16 * i + ROWS, 16)
            steer[slot, pl.ds(at, 16), :] = (weight * (u * horner(SIN, w))).astype(jnp.bfloat16)
            return carry

        lax.fori_loop(0, ROWS // 16, rows, 0)

    build(g)

    @pl.when(r > 0)
    def _():
        halo_copy(0, after).wait_recv()
        lay(halo.at[0], 0)

    @pl.when(r == 0)
    def _():
        et[:, 0:RD, :] = jnp.zeros((2, RD, 128), jnp.float32)

    @pl.when(r < NR - 1)
    def _():
        halo_copy(1, before).wait_recv()
        lay(halo.at[1], 2)

    @pl.when(r == NR - 1)
    def _():
        et[:, 2 * RD : 3 * RD, :] = jnp.zeros((2, RD, 128), jnp.float32)

    def copy(slot, piece, way, device):
        part = pl.ds(piece * PR, PR)
        return pltpu.make_async_remote_copy(
            gath.at[slot, part], gath.at[slot, part], ss.at[slot, piece, way], rs.at[slot, piece],
            device_id=device, device_id_type=MESH,
        )

    def send(slot, piece, entry, own):
        @pl.when((pos < 3) & (entry <= pos))
        def _():
            copy(slot, piece, 0, right).start()

        @pl.when((pos > 0) & (entry >= pos))
        def _():
            copy(slot, piece, 1, left).start()

        if own:
            copy(slot, piece, 2, across).start()
        copy(slot, piece, 3, other).start()

    quarter = lax.broadcasted_iota(jnp.int32, (BAND + RD, 128), 1) // C
    for b in range(2):
        picked = et[b, pl.ds(off_ref[4 * b] + HALO, BAND + RD), :]
        for q in range(1, 4):
            picked = jnp.where(quarter == q, et[b, pl.ds(off_ref[4 * b + q] + HALO, BAND + RD), :], picked)
        win[...] = picked
        for t in range(2):
            total = [jnp.zeros((8, 128), jnp.float32) for _ in range(8)]
            for k in range(BAND):
                tap = taps[b, pl.ds(k, 8, stride=0), :]
                for i in range(8):
                    total[i] = total[i] + tap * win[64 * t + 8 * i + k : 64 * t + 8 * i + k + 8, :]
            acc[64 * t : 64 * t + 64, :] = jnp.concatenate(total, axis=0)
        gath[g, b * 128 : (b + 1) * 128, :] = acc[0:RD, :].T.astype(jnp.bfloat16)
        send(g, b, pos, True)

    def add(slot, first=False):
        part = jnp.dot(steer[slot], gath[slot], preferred_element_type=jnp.float32)
        acc[...] = part if first else acc[...] + part

    add(g, True)

    def near(i):
        return (jnp.abs(pos - 1), 2 + pos // 2 - 2 * (pos // 3), 3 * (1 - pos // 2))[i]

    events = [(0, near(i)) for i in range(3)] + [(1, pos)] + [(1, near(i)) for i in range(3)]
    chips = [4 * (half if o == 0 else 1 - half) + entry for o, entry in events]

    def ready(slot):
        mine_copy(slot, 1).wait_recv()
        build(slot)

    ready(2 * z + 1 - core)

    def partner(chip):
        slot = 2 * chip + 1 - core
        for piece in range(NC):
            copy(slot, piece, 3, other).wait_recv()
        add(slot)

    previous = z
    for (o, entry), chip in zip(events, chips):
        slot = 2 * chip + core
        ready(slot)
        ready(2 * chip + 1 - core)
        for piece in range(NC):
            copy(slot, piece, 3, other).wait_recv()
            send(slot, piece, entry, False)
        partner(previous)
        add(slot)
        previous = chip
    partner(previous)

    re_ref[...] = acc[0:ROWS, :]
    im_ref[...] = acc[ROWS : 2 * ROWS, :]

    @pl.when(r < NR - 1)
    def _():
        halo_copy(0, after).wait_send()

    @pl.when(r > 0)
    def _():
        halo_copy(1, before).wait_send()

    for j in range(1, NP):
        mine_copy(g, j).wait_send()

    for (o, entry), chip in zip([(0, pos)] + events, [z] + chips):
        slot = 2 * chip + core
        for piece in range(NC):

            @pl.when((pos < 3) & (entry <= pos))
            def _():
                copy(slot, piece, 0, right).wait_send()

            @pl.when((pos > 0) & (entry >= pos))
            def _():
                copy(slot, piece, 1, left).wait_send()

            if chip is z:
                copy(slot, piece, 2, across).wait_send()
            copy(slot, piece, 3, other).wait_send()


def shards(echoes, band_offset, sway_delay, channel_gain, track_bin):
    whole = pl.BlockSpec(memory_space=pltpu.VMEM)
    scalars = pl.BlockSpec(memory_space=pltpu.SMEM)
    out = jax.ShapeDtypeStruct((ROWS, RD), jnp.float32)
    return pl.pallas_call(
        kernel,
        out_shape=(out, out),
        in_specs=[scalars, scalars, whole, whole, whole],
        out_specs=(whole, whole),
        scratch_shapes=[
            pltpu.VMEM((2, PC, RD), jnp.bfloat16),
            pltpu.VMEM((2, 3 * RD, 128), jnp.float32),
            pltpu.VMEM((BAND + RD, 128), jnp.float32),
            pltpu.VMEM((2, BAND, 128), jnp.float32),
            pltpu.VMEM((NP, PC, RD), jnp.bfloat16),
            pltpu.VMEM((NP, 8, PC), jnp.int32),
            pltpu.VMEM((NP, 2 * ROWS, PC), jnp.bfloat16),
            pltpu.VMEM((2 * ROWS, RD), jnp.float32),
            pltpu.SemaphoreType.DMA((2,)),
            pltpu.SemaphoreType.DMA((2,)),
            pltpu.SemaphoreType.DMA((NP,)),
            pltpu.SemaphoreType.DMA((NP,)),
            pltpu.SemaphoreType.DMA((NP, NC, 4)),
            pltpu.SemaphoreType.DMA((NP, NC)),
        ],
        compiler_params=pltpu.CompilerParams(collective_id=0, has_side_effects=True),
    )(band_offset, track_bin, echoes.reshape(PC, RD), sway_delay, channel_gain)


def solution(mesh):
    return jax.shard_map(
        shards,
        mesh=mesh,
        in_specs=(P("ping", None, "range"), P("ping"), P("ping", None), P("ping", None), P("ping")),
        out_specs=(P("ping", "range"), P("ping", "range")),
        check_vma=False,
    )
```

time: 186 us -> 58.3 us (0.31)
  waiting for transfers between devices: 111 us -> 0 us
  Pallas kernels: 0 us -> 54.6 us
  starting transfers between devices: 20.4 us -> 0 us
  matrix products: 19.4 us -> 0 us
  between operations: 14.2 us -> 0.65 us
  local copies, waits for them, and re-layouts: 12.8 us -> 2.14 us
  loops' own time: 4.8 us -> 0 us
    reduce_scatter x1 -> x0, waiting for transfers between devices: 111 us -> none  [shards(): lax.psum_scatter(whole.astype(jnp.bfloat16), 'ping', scatter_dimension=0,...]
    pallas_call x0 -> x1, Pallas kernels: none -> 54.6 us  [shards(): pl.pallas_call(kernel, out_shape=(out, out), in_specs=[scalars, scalars,...]
    ppermute x2 -> x0, starting transfers between devices: 20.4 us -> none  [the longest x1 16.9 us: extended(): lax.ppermute(lax.slice_in_dim(block, 0, width, axis=dim), axis, backward)]
    dot_general x16 -> x0, matrix products: 18.4 us -> none  [the longest x8 9.21 us: one_block(): part_imag = jnp.dot(steer_imag, columns, preferred_element_type=jnp.float32)]
    another operation x1 -> x0, loops' own time: 4.8 us -> none  [image_rows(): blocks = lax.map(one_block, jnp.arange(block_count, dtype=jnp.int32))]
    dynamic_slice x8 -> x0, local copies, waits for them, and re-layouts: 4.64 us -> none  [image_rows(): blocks = lax.map(one_block, jnp.arange(block_count, dtype=jnp.int32))]
    gather x2 -> x0, local copies, waits for them, and re-layouts: 1.99 us -> none  [pick(): return lax.dynamic_slice_in_dim(row, shift + HALO, samples + BAND - 1, 1)]
  transfers between devices with their start and end apart: 3 -> 0, of which waited for: 1 -> 0; matrix products, arithmetic and copies ran while one was open for 1% -> 0% of each run, Pallas kernels for 0% -> 0%
where the time goes in v1:
time: 58.3 us; the launch traced here: 57.4 us
  Pallas kernels  54.6 us (94%)
  local copies, waits for them, and re-layouts  2.14 us (4%)
  between operations  0.65 us (1%)
    pallas_call x1, Pallas kernels, shards(): pl.pallas_call(kernel, out_shape=(out, out), in_specs=[scalars, scalars,...  54.6 us
    unnamed x4, local copies, waits for them, and re-layouts  2.14 us

profile of v1, /device:TPU:6, one launch (start us, length us, event | category | flops | bytes accessed | tf_op | source)
XLA Modules:
  0.0 57.4 jit_solution(10513331105331308096)
XLA Ops:
  0.6 54.6 %shard_map.68 = (f32[128,128]{1,0:T(8,128)}, f32[128,128]{1,0:T(8,128)}) custom-call(s32[8]{0:T(128)} %off_ref.1, s32[8]{0:T(128)} %track_ref.1, bf16[256,128]{1,0:T(8,128)(2,1)} %bitcast.1, f32[8,32]{1,0:T(8,128)} %sway_ref.1, f32[8,32]{1,0:T(8,128)} %gain_ref.1), custom_call_target="tpu_custom_call" | custom-call | tf_op jit(solution)/shard_map/pallas_call | solution.py:276
  55.2 0.0 copy-start
  55.2 1.5 %copy.9 = f32[128,128]{1,0:T(8,128)} copy(f32[128,128]{1,0:T(8,128)} %get-tuple-element.4) | data formatting | bytes 131072
  56.7 0.0 copy-done
  56.7 0.6 %copy.10 = f32[128,128]{1,0:T(8,128)} copy(f32[128,128]{1,0:T(8,128)S(1)} %copy-done) | data formatting | bytes 131072
Async XLA Ops:
  55.2 1.5 %copy-start = (f32[128,128]{1,0:T(8,128)S(1)}, f32[128,128]{1,0:T(8,128)}, u32[]{:S(2)}) copy-start(f32[128,128]{1,0:T(8,128)} %get-tuple-element.5) | copy-start | bytes 196612

commit v2 on v1

v2 whole, which is shorter than its diff:
```python
import functools
import math

import jax
import jax.numpy as jnp
import numpy as np
from jax import lax
from jax.experimental import pallas as pl
from jax.experimental.pallas import tpu as pltpu
from jax.sharding import PartitionSpec as P

X = 2048
BAND = 64
HALO = 128
NR = 32
NP = 16
PD = 8
C = 32
RD = 128
PC = PD * C
ROWS = X // NP
GROUP = 8
NC = 2
PR = RD // NC
MESH = pl.DeviceIdType.MESH


def fit(fun, degree):
    nodes = 0.125 + 0.125 * np.cos(np.pi * (np.arange(400) + 0.5) / 400)
    series = np.polynomial.chebyshev.Chebyshev.fit(nodes, fun(nodes), degree, domain=[0.0, 0.25])
    return [float(c) for c in series.convert(kind=np.polynomial.Polynomial).coef]


COS = fit(lambda w: np.cos(2 * np.pi * np.sqrt(w)), 8)
SIN = fit(lambda w: np.sin(2 * np.pi * np.sqrt(w)) / np.sqrt(w), 7)
SINPI = fit(lambda w: np.sin(np.pi * np.sqrt(w)) / np.sqrt(w), 6)


def horner(coefs, w):
    value = jnp.full_like(w, coefs[-1])
    for c in coefs[-2::-1]:
        value = value * w + c
    return value


def sin_pi(u):
    u = jnp.minimum(u, 1.0 - u)
    return u * horner(SINPI, u * u)


def kernel(
    off_ref, track_ref, e_ref, sway_ref, gain_ref, re_ref, im_ref,
    halo, et, win, taps, mine, gath, steer, acc, out_a, out_b, in_a, in_b,
    hs, hr, ms, mr, ss, rs, xs, xr, bs, br,
):
    r = lax.axis_index("range")
    g = lax.axis_index("ping")
    y = r % 4
    half, q = g // GROUP, g % GROUP
    pos, core = q // 2, q % 2
    base = GROUP * half
    across = (r, g + GROUP - 2 * GROUP * half)
    after = (jnp.minimum(r + 1, NR - 1), g)
    before = (jnp.maximum(r - 1, 0), g)
    crossing = 1 // (y + 1) - 1 // (r + 1) + y // 3 - r // (NR - 1)
    beyond = jnp.clip(r - 1 + 2 * (y // 3), 0, NR - 1)
    far = ((beyond, g), (beyond, g + GROUP - 2 * GROUP * half))

    barrier = pltpu.get_barrier_semaphore()

    def greet(device):
        pl.semaphore_signal(barrier, 1, device_id=device, device_id_type=MESH)

    @pl.when(crossing == 1)
    def _():
        greet(far[0])
        greet(far[1])

    for j in range(1, GROUP):
        greet((r, base + (q + j) % GROUP))
    greet(across)

    @pl.when(y > 0)
    def _():
        greet(before)

    @pl.when(y < 3)
    def _():
        greet(after)

    lane = lax.broadcasted_iota(jnp.int32, (1, PC), 1)
    centre = lane % C
    for p in range(PD):
        centre = centre + jnp.where(lane // C == p, 2 * track_ref[p], 0)
    mine[q] = centre

    kpos = lax.broadcasted_iota(jnp.int32, (BAND, 1), 0).astype(jnp.float32)
    edge = sin_pi((kpos + 0.5) * (1.0 / BAND))
    edge = edge * edge
    kfull = lax.broadcasted_iota(jnp.int32, (BAND, 128), 0)
    odd = (kfull % 2).astype(jnp.float32)
    for b in range(2):
        sway = jnp.concatenate([sway_ref[4 * b + i : 4 * b + i + 1, :] for i in range(4)], axis=1)
        gain = jnp.concatenate([gain_ref[4 * b + i : 4 * b + i + 1, :] for i in range(4)], axis=1)
        top = sin_pi(sway) * (1.0 / math.pi)
        shift = kfull.astype(jnp.float32) - (BAND / 2 - 1) - sway
        sinc = jnp.where(shift == 0.0, 1.0, (1.0 - 2.0 * odd) * top / jnp.where(shift == 0.0, 1.0, shift))
        taps[b] = sinc * edge * gain

    zeros = jnp.zeros((RD, 128), jnp.float32)

    def lay(block, kind, third):
        for b in range(2):
            et[kind, b, third * RD : (third + 1) * RD, :] = block[b * 128 : (b + 1) * 128, :].astype(jnp.float32).T

    def blank(kind, third):
        for b in range(2):
            et[kind, b, third * RD : (third + 1) * RD, :] = zeros

    quarter = lax.broadcasted_iota(jnp.int32, (BAND + RD, 128), 1) // C

    def align(kind):
        for b in range(2):
            picked = et[kind, b, pl.ds(off_ref[4 * b] + HALO, BAND + RD), :]
            for i in range(1, 4):
                picked = jnp.where(quarter == i, et[kind, b, pl.ds(off_ref[4 * b + i] + HALO, BAND + RD), :], picked)
            win[b] = picked

    def filtered(kind, piece):
        for b in range(2):
            total = [jnp.zeros((8, 128), jnp.float32) for _ in range(PR // 8)]
            for k in range(BAND):
                tap = taps[b, pl.ds(k, 8, stride=0), :]
                for i in range(PR // 8):
                    at = PR * piece + 8 * i + k
                    total[i] = total[i] + tap * win[b, at : at + 8, :]
            block = jnp.concatenate(total, axis=0).astype(jnp.bfloat16)
            gath[kind, q, piece * PR : (piece + 1) * PR, b * 128 : (b + 1) * 128] = block

    lay(e_ref, 0, 1)
    blank(1, 1)

    @pl.when(y == 3)
    def _():
        lay(e_ref, 1, 0)
        blank(1, 2)

    @pl.when(y == 0)
    def _():
        blank(1, 0)
        lay(e_ref, 1, 2)

    @pl.when(crossing == 1)
    def _():
        align(1)
        for piece in range(NC):
            filtered(1, piece)

    pl.semaphore_wait(barrier, GROUP + 2 - 1 // (y + 1) - y // 3 + 2 * crossing)

    def halo_copy(way, device):
        return pltpu.make_async_remote_copy(
            e_ref, halo.at[way], hs.at[way], hr.at[way], device_id=device, device_id_type=MESH
        )

    @pl.when(y < 3)
    def _():
        halo_copy(0, after).start()

    @pl.when(y > 0)
    def _():
        halo_copy(1, before).start()

    def mine_copy(slot, j):
        return pltpu.make_async_remote_copy(
            mine.at[slot], mine.at[slot], ms.at[j], mr.at[slot],
            device_id=(r, base + (q + j) % GROUP), device_id_type=MESH,
        )

    for j in range(1, GROUP):
        mine_copy(q, j).start()

    def copy(kind, slot, piece, way):
        rows = pl.ds(piece * PR, PR)
        peer = q + 1 - 2 * core if way == 0 else (q + 2 * way) % GROUP
        return pltpu.make_async_remote_copy(
            gath.at[kind, slot, rows], gath.at[kind, slot, rows], ss.at[kind, slot, piece, way], rs.at[kind, slot, piece],
            device_id=(r, base + peer), device_id_type=MESH,
        )

    def spread(kind, piece):
        for way in (2, 1, 3, 0):
            copy(kind, q, piece, way).start()

    @pl.when(crossing == 1)
    def _():
        for piece in range(NC):
            spread(1, piece)

    @pl.when(y > 0)
    def _():
        halo_copy(0, after).wait_recv()
        lay(halo.at[0], 0, 0)

    @pl.when(y == 0)
    def _():
        blank(0, 0)

    @pl.when(y < 3)
    def _():
        halo_copy(1, before).wait_recv()
        lay(halo.at[1], 0, 2)

    @pl.when(y == 3)
    def _():
        blank(0, 2)

    align(0)
    for piece in range(NC):
        filtered(0, piece)
        spread(0, piece)

    scale = 1.0 / math.sqrt(NP * PC)

    def build(kind, slot, band):
        full = (64 * 2 * (2 * band + 65)).astype(jnp.float32)
        turn = 1.0 / jnp.full((16, PC), full, jnp.float32)
        row = 2 * lax.broadcasted_iota(jnp.int32, (16, PC), 0)
        from_centre = row - jnp.broadcast_to(mine[slot], (16, PC))

        def rows(i, carry):
            first = g + (i // 8) * (GROUP - 2 * GROUP * half)
            m = (from_centre + (2 * ROWS * first + 32 * (i % 8))).astype(jnp.float32)
            m2 = m * m
            u = (m2 - jnp.floor(m2 * turn + 0.5) * full) * turn
            w = u * u
            weight = jnp.exp(m2 * (-1.0 / (8.0 * 65536.0))) * scale
            at = 2 * ROWS * (i // 8) + 16 * (i % 8)
            steer[kind, slot, pl.ds(pl.multiple_of(at, 16), 16), :] = (weight * horner(COS, w)).astype(jnp.bfloat16)
            at = at + ROWS
            steer[kind, slot, pl.ds(pl.multiple_of(at, 16), 16), :] = (weight * (u * horner(SIN, w))).astype(
                jnp.bfloat16
            )
            return carry

        lax.fori_loop(0, 2 * ROWS // 16, rows, 0)

    def slots(way):
        return (q + 2 * way) % GROUP

    twin = q + 1 - 2 * core
    order = [q, twin] + [s for way in (1, 3, 2) for s in (slots(way), (twin + 2 * way) % GROUP)]

    for i, slot in enumerate(order):
        if i:
            mine_copy(slot, 1).wait_recv()

        @pl.when(crossing == 1)
        def _():
            build(1, slot, beyond)

        build(0, slot, r)

    def add(kind, slot, piece, first=False):
        part = lax.dot_general(
            gath[kind, slot, piece * PR : (piece + 1) * PR, :], steer[kind, slot],
            (((1,), (1,)), ((), ())), preferred_element_type=jnp.float32,
        )
        rows = slice(piece * PR, (piece + 1) * PR)
        acc[rows, :] = part if first else acc[rows, :] + part

    def gather(kind, piece):
        add(kind, q, piece, True)
        for way in (1, 3, 2):
            copy(kind, slots(way), piece, 0).wait_recv()
            copy(kind, slots(way), piece, 0).start()
            add(kind, slots(way), piece)
        for way in (0, 1, 3, 2):
            slot = (twin + 2 * way) % GROUP
            copy(kind, slot, piece, 0).wait_recv()
            add(kind, slot, piece)

    def across_copy(piece):
        return pltpu.make_async_remote_copy(
            out_a.at[piece], in_a.at[piece], xs.at[piece], xr.at[piece], device_id=across, device_id_type=MESH
        )

    def far_copy(piece, which):
        return pltpu.make_async_remote_copy(
            out_b.at[which, piece], in_b.at[which, piece], bs.at[which, piece], br.at[which, piece],
            device_id=far[which], device_id_type=MESH,
        )

    W = 2 * ROWS

    @pl.when(crossing == 1)
    def _():
        for piece in range(NC):
            gather(1, piece)
            for which in range(2):
                out_b[which, piece] = acc[piece * PR : (piece + 1) * PR, which * W : (which + 1) * W].astype(jnp.bfloat16)
                far_copy(piece, which).start()

    for piece in range(NC):
        gather(0, piece)
        out_a[piece] = acc[piece * PR : (piece + 1) * PR, W : 2 * W].astype(jnp.bfloat16)
        across_copy(piece).start()

    for piece in range(NC):
        rows = slice(piece * PR, (piece + 1) * PR)
        across_copy(piece).wait_recv()
        acc[rows, 0:W] = acc[rows, 0:W] + in_a[piece].astype(jnp.float32)

        @pl.when(crossing == 1)
        def _():
            for which in range(2):
                far_copy(piece, which).wait_recv()
                acc[rows, 0:W] = acc[rows, 0:W] + in_b[which, piece].astype(jnp.float32)

    re_ref[...] = acc[:, 0:ROWS].T
    im_ref[...] = acc[:, ROWS : 2 * ROWS].T

    @pl.when(y < 3)
    def _():
        halo_copy(0, after).wait_send()

    @pl.when(y > 0)
    def _():
        halo_copy(1, before).wait_send()

    for j in range(1, GROUP):
        mine_copy(q, j).wait_send()

    def left(kind):
        for piece in range(NC):
            for way in range(4):
                copy(kind, q, piece, way).wait_send()
                if way:
                    copy(kind, slots(way), piece, 0).wait_send()

    left(0)
    for piece in range(NC):
        across_copy(piece).wait_send()

    @pl.when(crossing == 1)
    def _():
        left(1)
        for piece in range(NC):
            for which in range(2):
                far_copy(piece, which).wait_send()


def shards(echoes, band_offset, sway_delay, channel_gain, track_bin):
    whole = pl.BlockSpec(memory_space=pltpu.VMEM)
    scalars = pl.BlockSpec(memory_space=pltpu.SMEM)
    out = jax.ShapeDtypeStruct((ROWS, RD), jnp.float32)
    dma = pltpu.SemaphoreType.DMA
    return pl.pallas_call(
        kernel,
        out_shape=(out, out),
        in_specs=[scalars, scalars, whole, whole, whole],
        out_specs=(whole, whole),
        scratch_shapes=[
            pltpu.VMEM((2, PC, RD), jnp.bfloat16),
            pltpu.VMEM((2, 2, 3 * RD, 128), jnp.float32),
            pltpu.VMEM((2, BAND + RD, 128), jnp.float32),
            pltpu.VMEM((2, BAND, 128), jnp.float32),
            pltpu.VMEM((GROUP, 1, PC), jnp.int32),
            pltpu.VMEM((2, GROUP, RD, PC), jnp.bfloat16),
            pltpu.VMEM((2, GROUP, 4 * ROWS, PC), jnp.bfloat16),
            pltpu.VMEM((RD, 4 * ROWS), jnp.float32),
            pltpu.VMEM((NC, PR, 2 * ROWS), jnp.bfloat16),
            pltpu.VMEM((2, NC, PR, 2 * ROWS), jnp.bfloat16),
            pltpu.VMEM((NC, PR, 2 * ROWS), jnp.bfloat16),
            pltpu.VMEM((2, NC, PR, 2 * ROWS), jnp.bfloat16),
            dma((2,)),
            dma((2,)),
            dma((GROUP,)),
            dma((GROUP,)),
            dma((2, GROUP, NC, 4)),
            dma((2, GROUP, NC)),
            dma((NC,)),
            dma((NC,)),
            dma((2, NC)),
            dma((2, NC)),
        ],
        compiler_params=pltpu.CompilerParams(collective_id=0, has_side_effects=True),
    )(band_offset, track_bin, echoes.reshape(PC, RD), sway_delay, channel_gain)


def solution(mesh):
    return jax.shard_map(
        shards,
        mesh=mesh,
        in_specs=(P("ping", None, "range"), P("ping"), P("ping", None), P("ping", None), P("ping")),
        out_specs=(P("ping", "range"), P("ping", "range")),
        check_vma=False,
    )
```

time: 58.3 us -> 52 us (0.89)
  Pallas kernels: 54.6 us -> 48.8 us
    pallas_call x1, Pallas kernels: 54.6 us -> 48.8 us  [shards(): pl.pallas_call(kernel, out_shape=(out, out), in_specs=[scalars, scalars,...]
where the time goes in v2:
time: 52 us; the launch traced here: 51.5 us
  Pallas kernels  48.8 us (94%)
  local copies, waits for them, and re-layouts  2.14 us (4%)
  between operations  0.65 us (1%)
    pallas_call x1, Pallas kernels, shards(): pl.pallas_call(kernel, out_shape=(out, out), in_specs=[scalars, scalars,...  48.8 us
    unnamed x4, local copies, waits for them, and re-layouts  2.14 us

profile of v2, /device:TPU:6, one launch (start us, length us, event | category | flops | bytes accessed | tf_op | source)
XLA Modules:
  0.0 51.5 jit_solution(12796660784044176608)
XLA Ops:
  0.6 48.8 %shard_map.68 = (f32[128,128]{1,0:T(8,128)}, f32[128,128]{1,0:T(8,128)}) custom-call(s32[8]{0:T(128)} %off_ref.1, s32[8]{0:T(128)} %track_ref.1, bf16[256,128]{1,0:T(8,128)(2,1)} %bitcast.1, f32[8,32]{1,0:T(8,128)} %sway_ref.1, f32[8,32]{1,0:T(8,128)} %gain_ref.1), custom_call_target="tpu_custom_call" | custom-call | tf_op jit(solution)/shard_map/pallas_call | solution.py:358
  49.4 0.0 copy-start
  49.4 1.5 %copy.9 = f32[128,128]{1,0:T(8,128)} copy(f32[128,128]{1,0:T(8,128)} %get-tuple-element.4) | data formatting | bytes 131072
  50.9 0.0 copy-done
  50.9 0.6 %copy.10 = f32[128,128]{1,0:T(8,128)} copy(f32[128,128]{1,0:T(8,128)S(1)} %copy-done) | data formatting | bytes 131072
Async XLA Ops:
  49.4 1.5 %copy-start = (f32[128,128]{1,0:T(8,128)S(1)}, f32[128,128]{1,0:T(8,128)}, u32[]{:S(2)}) copy-start(f32[128,128]{1,0:T(8,128)} %get-tuple-element.5) | copy-start | bytes 196612

commit v3 on v2

--- a/solution.py
+++ b/solution.py
@@ -20,7 +20,7 @@
 PC = PD * C
 ROWS = X // NP
 GROUP = 8
-NC = 2
+NC = 1
 PR = RD // NC
 MESH = pl.DeviceIdType.MESH
 
@@ -50,8 +50,8 @@
 
 def kernel(
     off_ref, track_ref, e_ref, sway_ref, gain_ref, re_ref, im_ref,
-    halo, et, win, taps, mine, gath, steer, acc, out_a, out_b, in_a, in_b,
-    hs, hr, ms, mr, ss, rs, xs, xr, bs, br,
+    halo, et, win, taps, mine, own_b, gath, steer, acc, out_a, in_a,
+    hs, hr, ms, mr, ss, rs, xs, xr, bs,
 ):
     r = lax.axis_index("range")
     g = lax.axis_index("ping")
@@ -64,7 +64,7 @@
     before = (jnp.maximum(r - 1, 0), g)
     crossing = 1 // (y + 1) - 1 // (r + 1) + y // 3 - r // (NR - 1)
     beyond = jnp.clip(r - 1 + 2 * (y // 3), 0, NR - 1)
-    far = ((beyond, g), (beyond, g + GROUP - 2 * GROUP * half))
+    far = (beyond, g + GROUP - 2 * GROUP * half)
 
     barrier = pltpu.get_barrier_semaphore()
 
@@ -73,12 +73,13 @@
 
     @pl.when(crossing == 1)
     def _():
-        greet(far[0])
-        greet(far[1])
-
+        greet(far)
+        for j in range(1, GROUP):
+            greet((r, GROUP - base + (q + j) % GROUP))
+
+    greet(across)
     for j in range(1, GROUP):
         greet((r, base + (q + j) % GROUP))
-    greet(across)
 
     @pl.when(y > 0)
     def _():
@@ -92,7 +93,7 @@
     centre = lane % C
     for p in range(PD):
         centre = centre + jnp.where(lane // C == p, 2 * track_ref[p], 0)
-    mine[q] = centre
+    mine[g] = centre
 
     kpos = lax.broadcasted_iota(jnp.int32, (BAND, 1), 0).astype(jnp.float32)
     edge = sin_pi((kpos + 0.5) * (1.0 / BAND))
@@ -135,7 +136,11 @@
                     at = PR * piece + 8 * i + k
                     total[i] = total[i] + tap * win[b, at : at + 8, :]
             block = jnp.concatenate(total, axis=0).astype(jnp.bfloat16)
-            gath[kind, q, piece * PR : (piece + 1) * PR, b * 128 : (b + 1) * 128] = block
+            rows, lanes = slice(piece * PR, (piece + 1) * PR), slice(b * 128, (b + 1) * 128)
+            if kind:
+                own_b[rows, lanes] = block
+            else:
+                gath[0, q, rows, lanes] = block
 
     lay(e_ref, 0, 1)
     blank(1, 1)
@@ -156,7 +161,7 @@
         for piece in range(NC):
             filtered(1, piece)
 
-    pl.semaphore_wait(barrier, GROUP + 2 - 1 // (y + 1) - y // 3 + 2 * crossing)
+    pl.semaphore_wait(barrier, GROUP + 2 - 1 // (y + 1) - y // 3 + GROUP * crossing)
 
     def halo_copy(way, device):
         return pltpu.make_async_remote_copy(
@@ -171,14 +176,27 @@
     def _():
         halo_copy(1, before).start()
 
-    def mine_copy(slot, j):
+    def mine_copy(group, there, j):
         return pltpu.make_async_remote_copy(
-            mine.at[slot], mine.at[slot], ms.at[j], mr.at[slot],
-            device_id=(r, base + (q + j) % GROUP), device_id_type=MESH,
-        )
+            mine.at[group], mine.at[group], ms.at[there, j], mr.at[group],
+            device_id=(r, base + there * (GROUP - 2 * base) + (q + j) % GROUP), device_id_type=MESH,
+        )
+
+    def far_copy(piece):
+        rows = pl.ds(piece * PR, PR)
+        return pltpu.make_async_remote_copy(
+            own_b.at[rows], gath.at[1, q, rows], bs.at[piece], rs.at[1, q, piece], device_id=far, device_id_type=MESH
+        )
+
+    @pl.when(crossing == 1)
+    def _():
+        for piece in range(NC):
+            far_copy(piece).start()
+        for j in range(GROUP):
+            mine_copy(g, 1, j).start()
 
     for j in range(1, GROUP):
-        mine_copy(q, j).start()
+        mine_copy(g, 0, j).start()
 
     def copy(kind, slot, piece, way):
         rows = pl.ds(piece * PR, PR)
@@ -192,11 +210,6 @@
         for way in (2, 1, 3, 0):
             copy(kind, q, piece, way).start()
 
-    @pl.when(crossing == 1)
-    def _():
-        for piece in range(NC):
-            spread(1, piece)
-
     @pl.when(y > 0)
     def _():
         halo_copy(0, after).wait_recv()
@@ -222,11 +235,14 @@
 
     scale = 1.0 / math.sqrt(NP * PC)
 
-    def build(kind, slot, band):
-        full = (64 * 2 * (2 * band + 65)).astype(jnp.float32)
+    def group_of(kind, slot):
+        return slot + base + kind * (GROUP - 2 * base)
+
+    def build(kind, slot):
+        full = (64 * 2 * (2 * r + 65)).astype(jnp.float32)
         turn = 1.0 / jnp.full((16, PC), full, jnp.float32)
         row = 2 * lax.broadcasted_iota(jnp.int32, (16, PC), 0)
-        from_centre = row - jnp.broadcast_to(mine[slot], (16, PC))
+        from_centre = row - jnp.broadcast_to(mine[group_of(kind, slot)], (16, PC))
 
         def rows(i, carry):
             first = g + (i // 8) * (GROUP - 2 * GROUP * half)
@@ -253,13 +269,8 @@
 
     for i, slot in enumerate(order):
         if i:
-            mine_copy(slot, 1).wait_recv()
-
-        @pl.when(crossing == 1)
-        def _():
-            build(1, slot, beyond)
-
-        build(0, slot, r)
+            mine_copy(group_of(0, slot), 0, 1).wait_recv()
+        build(0, slot)
 
     def add(kind, slot, piece, first=False):
         part = lax.dot_general(
@@ -269,12 +280,14 @@
         rows = slice(piece * PR, (piece + 1) * PR)
         acc[rows, :] = part if first else acc[rows, :] + part
 
-    def gather(kind, piece):
-        add(kind, q, piece, True)
+    def arrive(kind, piece):
         for way in (1, 3, 2):
             copy(kind, slots(way), piece, 0).wait_recv()
             copy(kind, slots(way), piece, 0).start()
-            add(kind, slots(way), piece)
+
+    def gather(kind, piece):
+        for way in (0, 1, 3, 2):
+            add(kind, slots(way), piece, kind == 0 and way == 0)
         for way in (0, 1, 3, 2):
             slot = (twin + 2 * way) % GROUP
             copy(kind, slot, piece, 0).wait_recv()
@@ -285,38 +298,44 @@
             out_a.at[piece], in_a.at[piece], xs.at[piece], xr.at[piece], device_id=across, device_id_type=MESH
         )
 
-    def far_copy(piece, which):
-        return pltpu.make_async_remote_copy(
-            out_b.at[which, piece], in_b.at[which, piece], bs.at[which, piece], br.at[which, piece],
-            device_id=far[which], device_id_type=MESH,
-        )
-
     W = 2 * ROWS
 
-    @pl.when(crossing == 1)
-    def _():
-        for piece in range(NC):
-            gather(1, piece)
-            for which in range(2):
-                out_b[which, piece] = acc[piece * PR : (piece + 1) * PR, which * W : (which + 1) * W].astype(jnp.bfloat16)
-                far_copy(piece, which).start()
+    def cross(piece):
+        out_a[piece] = acc[piece * PR : (piece + 1) * PR, W : 2 * W].astype(jnp.bfloat16)
+        across_copy(piece).start()
+
+    for piece in range(NC):
+        arrive(0, piece)
+
+    @pl.when(crossing == 1)
+    def _():
+        for piece in range(NC):
+            copy(1, q, piece, 0).wait_recv()
+            spread(1, piece)
 
     for piece in range(NC):
         gather(0, piece)
-        out_a[piece] = acc[piece * PR : (piece + 1) * PR, W : 2 * W].astype(jnp.bfloat16)
-        across_copy(piece).start()
+
+        @pl.when(crossing == 0)
+        def _():
+            cross(piece)
+
+    @pl.when(crossing == 1)
+    def _():
+        for slot in order:
+            mine_copy(group_of(1, slot), 0, 1).wait_recv()
+            build(1, slot)
+        for piece in range(NC):
+            arrive(1, piece)
+        for piece in range(NC):
+            gather(1, piece)
+            cross(piece)
 
     for piece in range(NC):
         rows = slice(piece * PR, (piece + 1) * PR)
         across_copy(piece).wait_recv()
         acc[rows, 0:W] = acc[rows, 0:W] + in_a[piece].astype(jnp.float32)
 
-        @pl.when(crossing == 1)
-        def _():
-            for which in range(2):
-                far_copy(piece, which).wait_recv()
-                acc[rows, 0:W] = acc[rows, 0:W] + in_b[which, piece].astype(jnp.float32)
-
     re_ref[...] = acc[:, 0:ROWS].T
     im_ref[...] = acc[:, ROWS : 2 * ROWS].T
 
@@ -329,7 +348,7 @@
         halo_copy(1, before).wait_send()
 
     for j in range(1, GROUP):
-        mine_copy(q, j).wait_send()
+        mine_copy(g, 0, j).wait_send()
 
     def left(kind):
         for piece in range(NC):
@@ -346,8 +365,9 @@
     def _():
         left(1)
         for piece in range(NC):
-            for which in range(2):
-                far_copy(piece, which).wait_send()
+            far_copy(piece).wait_send()
+        for j in range(GROUP):
+            mine_copy(g, 1, j).wait_send()
 
 
 def shards(echoes, band_offset, sway_delay, channel_gain, track_bin):
@@ -365,24 +385,22 @@
             pltpu.VMEM((2, 2, 3 * RD, 128), jnp.float32),
             pltpu.VMEM((2, BAND + RD, 128), jnp.float32),
             pltpu.VMEM((2, BAND, 128), jnp.float32),
-            pltpu.VMEM((GROUP, 1, PC), jnp.int32),
+            pltpu.VMEM((NP, 1, PC), jnp.int32),
+            pltpu.VMEM((RD, PC), jnp.bfloat16),
             pltpu.VMEM((2, GROUP, RD, PC), jnp.bfloat16),
             pltpu.VMEM((2, GROUP, 4 * ROWS, PC), jnp.bfloat16),
             pltpu.VMEM((RD, 4 * ROWS), jnp.float32),
             pltpu.VMEM((NC, PR, 2 * ROWS), jnp.bfloat16),
-            pltpu.VMEM((2, NC, PR, 2 * ROWS), jnp.bfloat16),
             pltpu.VMEM((NC, PR, 2 * ROWS), jnp.bfloat16),
-            pltpu.VMEM((2, NC, PR, 2 * ROWS), jnp.bfloat16),
             dma((2,)),
             dma((2,)),
-            dma((GROUP,)),
-            dma((GROUP,)),
+            dma((2, GROUP)),
+            dma((NP,)),
             dma((2, GROUP, NC, 4)),
             dma((2, GROUP, NC)),
             dma((NC,)),
             dma((NC,)),
-            dma((2, NC)),
-            dma((2, NC)),
+            dma((NC,)),
         ],
         compiler_params=pltpu.CompilerParams(collective_id=0, has_side_effects=True),
     )(band_offset, track_bin, echoes.reshape(PC, RD), sway_delay, channel_gain)

time: 52 us -> 48.5 us (0.933)
  Pallas kernels: 48.8 us -> 45.5 us
    pallas_call x1, Pallas kernels: 48.8 us -> 45.5 us  [shards(): pl.pallas_call(kernel, out_shape=(out, out), in_specs=[scalars, scalars,...]
where the time goes in v3:
time: 48.5 us; the launch traced here: 48.3 us
  Pallas kernels  45.5 us (94%)
  local copies, waits for them, and re-layouts  2.14 us (4%)
  between operations  0.65 us (1%)
    pallas_call x1, Pallas kernels, shards(): pl.pallas_call(kernel, out_shape=(out, out), in_specs=[scalars, scalars,...  45.5 us
    unnamed x4, local copies, waits for them, and re-layouts  2.14 us

profile of v3, /device:TPU:6, one launch (start us, length us, event | category | flops | bytes accessed | tf_op | source)
XLA Modules:
  0.0 48.3 jit_solution(12034758001499091772)
XLA Ops:
  0.6 45.5 %shard_map.68 = (f32[128,128]{1,0:T(8,128)}, f32[128,128]{1,0:T(8,128)}) custom-call(s32[8]{0:T(128)} %off_ref.1, s32[8]{0:T(128)} %track_ref.1, bf16[256,128]{1,0:T(8,128)(2,1)} %bitcast.1, f32[8,32]{1,0:T(8,128)} %sway_ref.1, f32[8,32]{1,0:T(8,128)} %gain_ref.1), custom_call_target="tpu_custom_call" | custom-call | tf_op jit(solution)/shard_map/pallas_call | solution.py:378
  46.2 0.0 copy-start
  46.2 1.5 %copy.9 = f32[128,128]{1,0:T(8,128)} copy(f32[128,128]{1,0:T(8,128)} %get-tuple-element.4) | data formatting | bytes 131072
  47.7 0.0 copy-done
  47.7 0.6 %copy.10 = f32[128,128]{1,0:T(8,128)} copy(f32[128,128]{1,0:T(8,128)S(1)} %copy-done) | data formatting | bytes 131072
Async XLA Ops:
  46.2 1.5 %copy-start = (f32[128,128]{1,0:T(8,128)S(1)}, f32[128,128]{1,0:T(8,128)}, u32[]{:S(2)}) copy-start(f32[128,128]{1,0:T(8,128)} %get-tuple-element.5) | copy-start | bytes 196612

commit v4 on v3

--- a/solution.py
+++ b/solution.py
@@ -49,8 +49,8 @@
 
 
 def kernel(
-    off_ref, track_ref, e_ref, sway_ref, gain_ref, re_ref, im_ref,
-    halo, et, win, taps, mine, own_b, gath, steer, acc, out_a, in_a,
+    off_in, track_in, e_in, sway_in, gain_in, re_ref, im_ref,
+    off_ref, track_ref, e_ref, sway_ref, gain_ref, loaded, halo, et, win, taps, mine, own_b, gath, steer, spin, head, acc, out_a, in_a,
     hs, hr, ms, mr, ss, rs, xs, xr, bs,
 ):
     r = lax.axis_index("range")
@@ -66,6 +66,11 @@
     beyond = jnp.clip(r - 1 + 2 * (y // 3), 0, NR - 1)
     far = (beyond, g + GROUP - 2 * GROUP * half)
 
+    pairs = ((track_in, track_ref), (off_in, off_ref), (e_in, e_ref), (sway_in, sway_ref), (gain_in, gain_ref))
+    loads = [pltpu.make_async_copy(a, b, loaded.at[i]) for i, (a, b) in enumerate(pairs)]
+    for load in loads:
+        load.start()
+
     barrier = pltpu.get_barrier_semaphore()
 
     def greet(device):
@@ -74,8 +79,6 @@
     @pl.when(crossing == 1)
     def _():
         greet(far)
-        for j in range(1, GROUP):
-            greet((r, GROUP - base + (q + j) % GROUP))
 
     greet(across)
     for j in range(1, GROUP):
@@ -88,6 +91,9 @@
     @pl.when(y < 3)
     def _():
         greet(after)
+
+    for load in loads:
+        load.wait()
 
     lane = lax.broadcasted_iota(jnp.int32, (1, PC), 1)
     centre = lane % C
@@ -161,7 +167,7 @@
         for piece in range(NC):
             filtered(1, piece)
 
-    pl.semaphore_wait(barrier, GROUP + 2 - 1 // (y + 1) - y // 3 + GROUP * crossing)
+    pl.semaphore_wait(barrier, GROUP + 2 - 1 // (y + 1) - y // 3 + crossing)
 
     def halo_copy(way, device):
         return pltpu.make_async_remote_copy(
@@ -176,10 +182,12 @@
     def _():
         halo_copy(1, before).start()
 
-    def mine_copy(group, there, j):
+    opposite = g + GROUP - 2 * base
+
+    def mine_copy(group, kind, j):
+        device = (r, base + (q + j) % GROUP) if j else across
         return pltpu.make_async_remote_copy(
-            mine.at[group], mine.at[group], ms.at[there, j], mr.at[group],
-            device_id=(r, base + there * (GROUP - 2 * base) + (q + j) % GROUP), device_id_type=MESH,
+            mine.at[group], mine.at[group], ms.at[kind, j], mr.at[group], device_id=device, device_id_type=MESH
         )
 
     def far_copy(piece):
@@ -192,8 +200,7 @@
     def _():
         for piece in range(NC):
             far_copy(piece).start()
-        for j in range(GROUP):
-            mine_copy(g, 1, j).start()
+        mine_copy(g, 1, 0).start()
 
     for j in range(1, GROUP):
         mine_copy(g, 0, j).start()
@@ -233,33 +240,67 @@
         filtered(0, piece)
         spread(0, piece)
 
+    @pl.when(crossing == 1)
+    def _():
+        mine_copy(opposite, 1, 0).wait_recv()
+        for j in range(1, GROUP):
+            mine_copy(opposite, 1, j).start()
+
     scale = 1.0 / math.sqrt(NP * PC)
 
     def group_of(kind, slot):
         return slot + base + kind * (GROUP - 2 * base)
 
+    full = (64 * 2 * (2 * r + 65)).astype(jnp.float32)
+
+    def wave(squares, factor):
+        turn = 1.0 / jnp.full(squares.shape, full, jnp.float32)
+        u = (squares - jnp.floor(squares * turn + 0.5) * full) * turn
+        w = u * u
+        weight = jnp.exp(squares * (-1.0 / (8.0 * 65536.0))) * factor
+        return weight * horner(COS, w), weight * (u * horner(SIN, w))
+
+    eight = lax.broadcasted_iota(jnp.int32, (128, 128), 0)
+    spin[0], spin[1] = wave((64 * (eight // 8) * (eight % 8)).astype(jnp.float32), 1.0)
+
     def build(kind, slot):
-        full = (64 * 2 * (2 * r + 65)).astype(jnp.float32)
-        turn = 1.0 / jnp.full((16, PC), full, jnp.float32)
-        row = 2 * lax.broadcasted_iota(jnp.int32, (16, PC), 0)
-        from_centre = row - jnp.broadcast_to(mine[group_of(kind, slot)], (16, PC))
-
-        def rows(i, carry):
-            first = g + (i // 8) * (GROUP - 2 * GROUP * half)
-            m = (from_centre + (2 * ROWS * first + 32 * (i % 8))).astype(jnp.float32)
-            m2 = m * m
-            u = (m2 - jnp.floor(m2 * turn + 0.5) * full) * turn
-            w = u * u
-            weight = jnp.exp(m2 * (-1.0 / (8.0 * 65536.0))) * scale
-            at = 2 * ROWS * (i // 8) + 16 * (i % 8)
-            steer[kind, slot, pl.ds(pl.multiple_of(at, 16), 16), :] = (weight * horner(COS, w)).astype(jnp.bfloat16)
-            at = at + ROWS
-            steer[kind, slot, pl.ds(pl.multiple_of(at, 16), 16), :] = (weight * (u * horner(SIN, w))).astype(
-                jnp.bfloat16
-            )
+        centres = mine[group_of(kind, slot)]
+        starts = [2 * ROWS * g - centres, 2 * ROWS * opposite - centres]
+        step = lax.broadcasted_iota(jnp.int32, (16, PC), 0)
+        n = jnp.concatenate([16 * step + start for start in starts], axis=0).astype(jnp.float32)
+        head[0], head[1] = wave(n * n, scale)
+        s8 = lax.broadcasted_iota(jnp.int32, (8, PC), 0)
+        turned = jnp.concatenate([4 * s8 * (start + s8) for start in starts], axis=0).astype(jnp.float32)
+        cos, sin = wave(turned, 1.0)
+        for part in range(2):
+            cos8, sin8 = cos[8 * part : 8 * part + 8], sin[8 * part : 8 * part + 8]
+
+            for i in range(ROWS // 16):
+                real, imag = [], []
+                for j in range(2):
+                    at = 16 * i + 8 * j
+                    cr = jnp.concatenate([spin[0, at : at + 8, :]] * 2, axis=1)
+                    ci = jnp.concatenate([spin[1, at : at + 8, :]] * 2, axis=1)
+                    br, bi = cos8 * cr - sin8 * ci, cos8 * ci + sin8 * cr
+                    hr = head[0, pl.ds(16 * part + 2 * i + j, 8, stride=0), :]
+                    hi = head[1, pl.ds(16 * part + 2 * i + j, 8, stride=0), :]
+                    real.append(hr * br - hi * bi)
+                    imag.append(hr * bi + hi * br)
+                at = 2 * ROWS * part + 16 * i
+                steer[kind, slot, at : at + 16, :] = jnp.concatenate(real, axis=0).astype(jnp.bfloat16)
+                at = at + ROWS
+                steer[kind, slot, at : at + 16, :] = jnp.concatenate(imag, axis=0).astype(jnp.bfloat16)
+
+    def build_all(kind):
+        for i, slot in enumerate(order):
+            if i:
+                mine_copy(group_of(kind, slot), 0, 1).wait_recv()
+
+        def one(slot, carry):
+            build(kind, slot)
             return carry
 
-        lax.fori_loop(0, 2 * ROWS // 16, rows, 0)
+        lax.fori_loop(0, GROUP, one, 0)
 
     def slots(way):
         return (q + 2 * way) % GROUP
@@ -267,42 +308,40 @@
     twin = q + 1 - 2 * core
     order = [q, twin] + [s for way in (1, 3, 2) for s in (slots(way), (twin + 2 * way) % GROUP)]
 
-    for i, slot in enumerate(order):
-        if i:
-            mine_copy(group_of(0, slot), 0, 1).wait_recv()
-        build(0, slot)
-
-    def add(kind, slot, piece, first=False):
-        part = lax.dot_general(
-            gath[kind, slot, piece * PR : (piece + 1) * PR, :], steer[kind, slot],
+    build_all(0)
+
+    def add(part, kind, slot, first=False):
+        product = lax.dot_general(
+            gath[kind, slot], steer[kind, slot, 2 * ROWS * part : 2 * ROWS * (part + 1), :],
             (((1,), (1,)), ((), ())), preferred_element_type=jnp.float32,
         )
-        rows = slice(piece * PR, (piece + 1) * PR)
-        acc[rows, :] = part if first else acc[rows, :] + part
+        acc[part] = product if first else acc[part] + product
 
     def arrive(kind, piece):
         for way in (1, 3, 2):
             copy(kind, slots(way), piece, 0).wait_recv()
             copy(kind, slots(way), piece, 0).start()
 
-    def gather(kind, piece):
+    def outer(kind):
         for way in (0, 1, 3, 2):
-            add(kind, slots(way), piece, kind == 0 and way == 0)
+            add(1, kind, slots(way), kind == 0 and way == 0)
         for way in (0, 1, 3, 2):
             slot = (twin + 2 * way) % GROUP
-            copy(kind, slot, piece, 0).wait_recv()
-            add(kind, slot, piece)
-
-    def across_copy(piece):
-        return pltpu.make_async_remote_copy(
-            out_a.at[piece], in_a.at[piece], xs.at[piece], xr.at[piece], device_id=across, device_id_type=MESH
-        )
-
-    W = 2 * ROWS
-
-    def cross(piece):
-        out_a[piece] = acc[piece * PR : (piece + 1) * PR, W : 2 * W].astype(jnp.bfloat16)
-        across_copy(piece).start()
+            for piece in range(NC):
+                copy(kind, slot, piece, 0).wait_recv()
+            add(1, kind, slot)
+
+    def inner(kind):
+        for i, slot in enumerate(order):
+            add(0, kind, slot, kind == 0 and i == 0)
+
+    across_copy = pltpu.make_async_remote_copy(
+        out_a, in_a, xs.at[0], xr.at[0], device_id=across, device_id_type=MESH
+    )
+
+    def cross():
+        out_a[...] = acc[1].astype(jnp.bfloat16)
+        across_copy.start()
 
     for piece in range(NC):
         arrive(0, piece)
@@ -312,32 +351,29 @@
         for piece in range(NC):
             copy(1, q, piece, 0).wait_recv()
             spread(1, piece)
-
-    for piece in range(NC):
-        gather(0, piece)
-
-        @pl.when(crossing == 0)
-        def _():
-            cross(piece)
-
-    @pl.when(crossing == 1)
-    def _():
-        for slot in order:
-            mine_copy(group_of(1, slot), 0, 1).wait_recv()
-            build(1, slot)
+        build_all(1)
+
+    outer(0)
+
+    @pl.when(crossing == 0)
+    def _():
+        cross()
+
+    inner(0)
+
+    @pl.when(crossing == 1)
+    def _():
         for piece in range(NC):
             arrive(1, piece)
-        for piece in range(NC):
-            gather(1, piece)
-            cross(piece)
-
-    for piece in range(NC):
-        rows = slice(piece * PR, (piece + 1) * PR)
-        across_copy(piece).wait_recv()
-        acc[rows, 0:W] = acc[rows, 0:W] + in_a[piece].astype(jnp.float32)
-
-    re_ref[...] = acc[:, 0:ROWS].T
-    im_ref[...] = acc[:, ROWS : 2 * ROWS].T
+        outer(1)
+        cross()
+        inner(1)
+
+    across_copy.wait_recv()
+    acc[0] = acc[0] + in_a[...].astype(jnp.float32)
+
+    re_ref[...] = acc[0, :, 0:ROWS].T
+    im_ref[...] = acc[0, :, ROWS : 2 * ROWS].T
 
     @pl.when(y < 3)
     def _():
@@ -358,29 +394,35 @@
                     copy(kind, slots(way), piece, 0).wait_send()
 
     left(0)
-    for piece in range(NC):
-        across_copy(piece).wait_send()
+    across_copy.wait_send()
 
     @pl.when(crossing == 1)
     def _():
         left(1)
         for piece in range(NC):
             far_copy(piece).wait_send()
-        for j in range(GROUP):
-            mine_copy(g, 1, j).wait_send()
+        mine_copy(g, 1, 0).wait_send()
+        for j in range(1, GROUP):
+            mine_copy(opposite, 1, j).wait_send()
 
 
 def shards(echoes, band_offset, sway_delay, channel_gain, track_bin):
     whole = pl.BlockSpec(memory_space=pltpu.VMEM)
-    scalars = pl.BlockSpec(memory_space=pltpu.SMEM)
+    kept = pl.BlockSpec(memory_space=pltpu.HBM)
     out = jax.ShapeDtypeStruct((ROWS, RD), jnp.float32)
     dma = pltpu.SemaphoreType.DMA
     return pl.pallas_call(
         kernel,
         out_shape=(out, out),
-        in_specs=[scalars, scalars, whole, whole, whole],
+        in_specs=[kept] * 5,
         out_specs=(whole, whole),
         scratch_shapes=[
+            pltpu.SMEM((PD,), jnp.int32),
+            pltpu.SMEM((PD,), jnp.int32),
+            pltpu.VMEM((PC, RD), jnp.bfloat16),
+            pltpu.VMEM((PD, C), jnp.float32),
+            pltpu.VMEM((PD, C), jnp.float32),
+            dma((5,)),
             pltpu.VMEM((2, PC, RD), jnp.bfloat16),
             pltpu.VMEM((2, 2, 3 * RD, 128), jnp.float32),
             pltpu.VMEM((2, BAND + RD, 128), jnp.float32),
@@ -389,17 +431,19 @@
             pltpu.VMEM((RD, PC), jnp.bfloat16),
             pltpu.VMEM((2, GROUP, RD, PC), jnp.bfloat16),
             pltpu.VMEM((2, GROUP, 4 * ROWS, PC), jnp.bfloat16),
-            pltpu.VMEM((RD, 4 * ROWS), jnp.float32),
-            pltpu.VMEM((NC, PR, 2 * ROWS), jnp.bfloat16),
-            pltpu.VMEM((NC, PR, 2 * ROWS), jnp.bfloat16),
+            pltpu.VMEM((2, 128, 128), jnp.float32),
+            pltpu.VMEM((2, 32, PC), jnp.float32),
+            pltpu.VMEM((2, RD, 2 * ROWS), jnp.float32),
+            pltpu.VMEM((RD, 2 * ROWS), jnp.bfloat16),
+            pltpu.VMEM((RD, 2 * ROWS), jnp.bfloat16),
             dma((2,)),
             dma((2,)),
             dma((2, GROUP)),
             dma((NP,)),
             dma((2, GROUP, NC, 4)),
             dma((2, GROUP, NC)),
-            dma((NC,)),
-            dma((NC,)),
+            dma((1,)),
+            dma((1,)),
             dma((NC,)),
         ],
         compiler_params=pltpu.CompilerParams(collective_id=0, has_side_effects=True),

time: 48.5 us -> 47.9 us (0.988)
  Pallas kernels: 45.5 us -> 44.7 us
    pallas_call x1, Pallas kernels: 45.5 us -> 44.7 us  [shards(): pl.pallas_call(kernel, out_shape=(out, out), in_specs=[kept] * 5, out_spe...]
where the time goes in v4:
time: 47.9 us; the launch traced here: 47.5 us
  Pallas kernels  44.7 us (93%)
  local copies, waits for them, and re-layouts  2.14 us (4%)
  between operations  0.65 us (1%)
    pallas_call x1, Pallas kernels, shards(): pl.pallas_call(kernel, out_shape=(out, out), in_specs=[kept] * 5, out_spe...  44.7 us
    unnamed x4, local copies, waits for them, and re-layouts  2.14 us

profile of v4, /device:TPU:6, one launch (start us, length us, event | category | flops | bytes accessed | tf_op | source)
XLA Modules:
  0.0 47.5 jit_solution(11672905040599911133)
XLA Ops:
  0.6 44.7 %shard_map.68 = (f32[128,128]{1,0:T(8,128)}, f32[128,128]{1,0:T(8,128)}) custom-call(s32[8]{0:T(128)} %off_in.1, s32[8]{0:T(128)} %track_in.1, bf16[256,128]{1,0:T(8,128)(2,1)} %bitcast.1, f32[8,32]{1,0:T(8,128)} %sway_in.1, f32[8,32]{1,0:T(8,128)} %gain_in.1), custom_call_target="tpu_custom_call" | custom-call | tf_op jit(solution)/shard_map/pallas_call | solution.py:414
  45.3 0.0 copy-start
  45.3 1.5 %copy.9 = f32[128,128]{1,0:T(8,128)} copy(f32[128,128]{1,0:T(8,128)} %get-tuple-element.4) | data formatting | bytes 131072
  46.8 0.0 copy-done
  46.8 0.6 %copy.10 = f32[128,128]{1,0:T(8,128)} copy(f32[128,128]{1,0:T(8,128)S(1)} %copy-done) | data formatting | bytes 131072
Async XLA Ops:
  45.3 1.5 %copy-start = (f32[128,128]{1,0:T(8,128)S(1)}, f32[128,128]{1,0:T(8,128)}, u32[]{:S(2)}) copy-start(f32[128,128]{1,0:T(8,128)} %get-tuple-element.5) | copy-start | bytes 196612

commit v5 on v4

--- a/solution.py
+++ b/solution.py
@@ -49,7 +49,7 @@
 
 
 def kernel(
-    off_in, track_in, e_in, sway_in, gain_in, re_ref, im_ref,
+    off_in, track_in, e_in, sway_in, gain_in, image_ref,
     off_ref, track_ref, e_ref, sway_ref, gain_ref, loaded, halo, et, win, taps, mine, own_b, gath, steer, spin, head, acc, out_a, in_a,
     hs, hr, ms, mr, ss, rs, xs, xr, bs,
 ):
@@ -68,9 +68,6 @@
 
     pairs = ((track_in, track_ref), (off_in, off_ref), (e_in, e_ref), (sway_in, sway_ref), (gain_in, gain_ref))
     loads = [pltpu.make_async_copy(a, b, loaded.at[i]) for i, (a, b) in enumerate(pairs)]
-    for load in loads:
-        load.start()
-
     barrier = pltpu.get_barrier_semaphore()
 
     def greet(device):
@@ -92,6 +89,8 @@
     def _():
         greet(after)
 
+    for load in loads:
+        load.start()
     for load in loads:
         load.wait()
 
@@ -174,14 +173,6 @@
             e_ref, halo.at[way], hs.at[way], hr.at[way], device_id=device, device_id_type=MESH
         )
 
-    @pl.when(y < 3)
-    def _():
-        halo_copy(0, after).start()
-
-    @pl.when(y > 0)
-    def _():
-        halo_copy(1, before).start()
-
     opposite = g + GROUP - 2 * base
 
     def mine_copy(group, kind, j):
@@ -201,6 +192,14 @@
         for piece in range(NC):
             far_copy(piece).start()
         mine_copy(g, 1, 0).start()
+
+    @pl.when(y < 3)
+    def _():
+        halo_copy(0, after).start()
+
+    @pl.when(y > 0)
+    def _():
+        halo_copy(1, before).start()
 
     for j in range(1, GROUP):
         mine_copy(g, 0, j).start()
@@ -369,12 +368,6 @@
         cross()
         inner(1)
 
-    across_copy.wait_recv()
-    acc[0] = acc[0] + in_a[...].astype(jnp.float32)
-
-    re_ref[...] = acc[0, :, 0:ROWS].T
-    im_ref[...] = acc[0, :, ROWS : 2 * ROWS].T
-
     @pl.when(y < 3)
     def _():
         halo_copy(0, after).wait_send()
@@ -394,7 +387,6 @@
                     copy(kind, slots(way), piece, 0).wait_send()
 
     left(0)
-    across_copy.wait_send()
 
     @pl.when(crossing == 1)
     def _():
@@ -405,17 +397,24 @@
         for j in range(1, GROUP):
             mine_copy(opposite, 1, j).wait_send()
 
+    across_copy.wait_recv()
+    acc[0] = acc[0] + in_a[...].astype(jnp.float32)
+
+    image_ref[0] = acc[0, :, 0:ROWS].T
+    image_ref[1] = acc[0, :, ROWS : 2 * ROWS].T
+    across_copy.wait_send()
+
 
 def shards(echoes, band_offset, sway_delay, channel_gain, track_bin):
     whole = pl.BlockSpec(memory_space=pltpu.VMEM)
     kept = pl.BlockSpec(memory_space=pltpu.HBM)
-    out = jax.ShapeDtypeStruct((ROWS, RD), jnp.float32)
+    out = jax.ShapeDtypeStruct((2, ROWS, RD), jnp.float32)
     dma = pltpu.SemaphoreType.DMA
-    return pl.pallas_call(
+    image = pl.pallas_call(
         kernel,
-        out_shape=(out, out),
+        out_shape=out,
         in_specs=[kept] * 5,
-        out_specs=(whole, whole),
+        out_specs=whole,
         scratch_shapes=[
             pltpu.SMEM((PD,), jnp.int32),
             pltpu.SMEM((PD,), jnp.int32),
@@ -448,6 +447,7 @@
         ],
         compiler_params=pltpu.CompilerParams(collective_id=0, has_side_effects=True),
     )(band_offset, track_bin, echoes.reshape(PC, RD), sway_delay, channel_gain)
+    return (image[0], image[1])
 
 
 def solution(mesh):

time: 47.9 us -> 47.2 us (0.985)
  local copies, waits for them, and re-layouts: 2.14 us -> 1.53 us
    unnamed x4 -> x0, local copies, waits for them, and re-layouts: 2.14 us -> none
    squeeze x0 -> x1, local copies, waits for them, and re-layouts: none -> 1.53 us  [shards(): return (image[0], image[1])]
where the time goes in v5:
time: 47.2 us; the launch traced here: 46.8 us
  Pallas kernels  44.6 us (94%)
  local copies, waits for them, and re-layouts  1.53 us (3%)
  between operations  0.64 us (1%)
    pallas_call x1, Pallas kernels, shards(): pl.pallas_call(kernel, out_shape=out, in_specs=[kept] * 5, out_specs=whol...  44.6 us
    squeeze x1, local copies, waits for them, and re-layouts, shards(): return (image[0], image[1])  1.53 us

profile of v5, /device:TPU:6, one launch (start us, length us, event | category | flops | bytes accessed | tf_op | source)
XLA Modules:
  0.0 46.8 jit_solution(6608823243625144316)
XLA Ops:
  0.6 44.6 %shard_map.68 = f32[2,128,128]{2,1,0:T(8,128)} custom-call(s32[8]{0:T(128)} %off_in.1, s32[8]{0:T(128)} %track_in.1, bf16[256,128]{1,0:T(8,128)(2,1)} %bitcast.5, f32[8,32]{1,0:T(8,128)} %sway_in.1, f32[8,32]{1,0:T(8,128)} %gain_in.1), custom_call_target="tpu_custom_call" | custom-call | tf_op jit(solution)/shard_map/pallas_call | solution.py:413
  45.3 1.5 %slice_bitcast_fusion = (f32[128,128]{1,0:T(8,128)}, f32[128,128]{1,0:T(8,128)}) fusion(f32[2,128,128]{2,1,0:T(8,128)} %shard_map.68), kind=kLoop, calls=%fused_computation | loop fusion | bytes 262144 | tf_op jit(solution)/shard_map/squeeze | solution.py:450

commit v6 on v5

--- a/solution.py
+++ b/solution.py
@@ -342,14 +342,17 @@
         out_a[...] = acc[1].astype(jnp.bfloat16)
         across_copy.start()
 
+    @pl.when(crossing == 1)
+    def _():
+        for piece in range(NC):
+            copy(1, q, piece, 0).wait_recv()
+            spread(1, piece)
+
     for piece in range(NC):
         arrive(0, piece)
 
     @pl.when(crossing == 1)
     def _():
-        for piece in range(NC):
-            copy(1, q, piece, 0).wait_recv()
-            spread(1, piece)
         build_all(1)
 
     outer(0)

time: 47.2 us -> 46.9 us (level)
  no operation moved by 1% of the time
where the time goes in v6:
time: 46.9 us; the launch traced here: 46.4 us
  Pallas kernels  44.3 us (94%)
  local copies, waits for them, and re-layouts  1.53 us (3%)
  between operations  0.64 us (1%)
    pallas_call x1, Pallas kernels, shards(): pl.pallas_call(kernel, out_shape=out, in_specs=[kept] * 5, out_specs=whol...  44.3 us
    squeeze x1, local copies, waits for them, and re-layouts, shards(): return (image[0], image[1])  1.53 us

profile of v6, /device:TPU:6, one launch (start us, length us, event | category | flops | bytes accessed | tf_op | source)
XLA Modules:
  0.0 46.4 jit_solution(764382959535250122)
XLA Ops:
  0.6 44.3 %shard_map.68 = f32[2,128,128]{2,1,0:T(8,128)} custom-call(s32[8]{0:T(128)} %off_in.1, s32[8]{0:T(128)} %track_in.1, bf16[256,128]{1,0:T(8,128)(2,1)} %bitcast.5, f32[8,32]{1,0:T(8,128)} %sway_in.1, f32[8,32]{1,0:T(8,128)} %gain_in.1), custom_call_target="tpu_custom_call" | custom-call | tf_op jit(solution)/shard_map/pallas_call | solution.py:416
  44.9 1.5 %slice_bitcast_fusion = (f32[128,128]{1,0:T(8,128)}, f32[128,128]{1,0:T(8,128)}) fusion(f32[2,128,128]{2,1,0:T(8,128)} %shard_map.68), kind=kLoop, calls=%fused_computation | loop fusion | bytes 262144 | tf_op jit(solution)/shard_map/squeeze | solution.py:453
